TPU v7x, 256 devices: a whole 4x4x8 slice. The times are simulated.
256 devices in a mesh: pipe: 4 (over y), fsdp: 32 (over x_hi, z, core), tensor: 2 (over x_lo).
Axes of the slice: x: 4 (x_hi: 2, x_lo: 2; x = x_hi * 2 + x_lo), y: 4, z: 8, core: 2. Of those that a mesh axis runs over, the one named last changes fastest.
Arguments:
- tokens: bfloat16 [6144, 4096], P('fsdp', 'tensor'), may hold values from -8 to 8
- norm_gains: float32 [4, 4096], P('pipe'), may hold values from 0.1 to 1.9
- q_blocks: bfloat16 [4, 4, 16, 256, 256], P('pipe', None, 'tensor', 'fsdp'), may hold values from -1 to 1
- k_blocks: bfloat16 [4, 4, 16, 256, 256], P('pipe', None, 'tensor', 'fsdp'), may hold values from -1 to 1
- v_blocks: bfloat16 [4, 4, 16, 256, 256], P('pipe', None, 'tensor', 'fsdp'), may hold values from -0.1875 to 0.1875
- o_blocks: bfloat16 [4, 4, 16, 256, 256], P('pipe', 'tensor', None, 'fsdp'), may hold values from -0.1875 to 0.1875
- q_rows: int32 [4, 4, 16], P('pipe', None, 'tensor'), may hold values from 0 to 15, as said below
- k_rows: int32 [4, 4, 16], P('pipe', None, 'tensor'), may hold values from 0 to 15, as said below
- v_rows: int32 [4, 4, 16], P('pipe', None, 'tensor'), may hold values from 0 to 15, as said below
- o_rows: int32 [4, 4, 16], P('pipe', 'tensor'), may hold values from 0 to 7, as said below
- mask_blocks: int32 [96, 4, 4], P('fsdp'), may hold values from 0 to 1, as said below
Outputs:
- activations: bfloat16 [4, 6144, 4096], P('pipe', 'fsdp', 'tensor')
Inputs may be any that keep to these rules, and one draw needn't show every extreme that they name: `q_rows`: for each section and column block the 4 listed input blocks are distinct. `k_rows`: for each section and column block the 4 listed input blocks are distinct. `v_rows`: for each section and column block the 4 listed input blocks are distinct. `o_rows`: entries k and k2 with k // 2 == k2 // 2 name distinct head blocks of one column block. Every diagonal block mask_blocks[n, i, i] is 1.
All inputs are finite; a program needn't handle non-finite values.
Results may differ from a plain program's by a relative error of at most 0.017.
Values may be sent and summed in bfloat16 or wider, within the bound.
A program may use at most 64 MiB of HBM per device.

v0:
```python
import jax
import jax.numpy as jnp
from jax import lax
from jax.sharding import PartitionSpec as P

HD = 128
MBLK = 16


def from_behind(value, axis, steps):
    count = lax.axis_size(axis)
    initial, last = (max(0, -steps), min(count, count - steps))
    return lax.ppermute(value, axis, [(source, source + steps) for source in range(initial, last)])


def block_project(in_rows, blocks, pattern):
    row_count = in_rows.shape[0]
    block_width = blocks.shape[-1]
    row_blocks = in_rows.reshape(row_count, -1, block_width)
    picked = row_blocks[:, pattern]
    product = jnp.einsum("rpcb,pcbe->rce", picked, blocks, preferred_element_type=jnp.float32)
    return product.reshape(row_count, -1)


def run_layer(
    u_half, mask_now, gain_row, q_full, k_full, v_full, out_weights, q_rows, k_rows, v_rows, o_rows
):
    gathered = lax.all_gather(u_half, "tensor", axis=1, tiled=True)
    values = gathered.astype(jnp.float32)
    inv_rms = lax.rsqrt(jnp.mean(values * values, axis=-1, keepdims=True) + 1e-05)
    normed = (values * inv_rms * gain_row[None, :]).astype(jnp.bfloat16)
    queries = block_project(normed, q_full, q_rows).astype(jnp.bfloat16)
    keys_proj = block_project(normed, k_full, k_rows).astype(jnp.bfloat16)
    values_proj = block_project(normed, v_full, v_rows).astype(jnp.bfloat16)
    o_full = out_weights()
    row_count = queries.shape[0]
    head_count = queries.shape[1] // HD
    head_shape = (row_count, head_count, HD)
    scores = jnp.einsum(
        "qhd,khd->hqk",
        queries.reshape(head_shape),
        keys_proj.reshape(head_shape),
        preferred_element_type=jnp.float32,
    ) * HD ** (-0.5)
    allowed = jnp.repeat(jnp.repeat(mask_now, MBLK, axis=0), MBLK, axis=1) == 1
    scores = jnp.where(allowed[None], scores, jnp.float32(-1e30))
    row_max = jnp.max(scores, axis=-1, keepdims=True)
    exp_scores = jnp.exp(scores - row_max)
    probs = (exp_scores / jnp.sum(exp_scores, axis=-1, keepdims=True)).astype(jnp.bfloat16)
    attended = jnp.einsum(
        "hqk,khd->qhd", probs, values_proj.reshape(head_shape), preferred_element_type=jnp.float32
    )
    attended = attended.astype(jnp.bfloat16).reshape(row_count, head_count * HD)
    partial_out = block_project(attended, o_full, o_rows)
    branch = lax.psum_scatter(
        partial_out.astype(jnp.bfloat16), "tensor", scatter_dimension=1, tiled=True
    ).astype(jnp.float32)
    return (u_half.astype(jnp.float32) + branch).astype(jnp.bfloat16)


def body(
    tokens,
    norm_gains,
    q_blocks,
    k_blocks,
    v_blocks,
    o_blocks,
    q_rows,
    k_rows,
    v_rows,
    o_rows,
    mask_blocks,
):
    sections = lax.axis_size("pipe")
    segment_idx = lax.axis_index("pipe")
    micro_count = mask_blocks.shape[0]
    seq_len = tokens.shape[0] // micro_count
    half_width = tokens.shape[1]
    q_full, k_full, v_full, o_all = (
        lax.all_gather(q_blocks, "fsdp", axis=3, tiled=True),
        lax.all_gather(k_blocks, "fsdp", axis=3, tiled=True),
        lax.all_gather(v_blocks, "fsdp", axis=3, tiled=True),
        lax.all_gather(o_blocks, "fsdp", axis=3, tiled=True),
    )

    def out_weights():
        return o_all[0]

    results = jnp.zeros((micro_count * seq_len, half_width), jnp.bfloat16)
    incoming = jnp.zeros((seq_len, half_width), jnp.bfloat16)
    total_steps = micro_count + sections - 1
    for step_idx in range(total_steps):
        if step_idx < micro_count:
            fresh_rows = tokens[step_idx * seq_len : (step_idx + 1) * seq_len]
        else:
            fresh_rows = jnp.zeros_like(incoming)
        u_half = jnp.where(segment_idx == 0, fresh_rows, incoming)
        offset = step_idx - segment_idx
        slot_idx = jnp.clip(offset, 0, micro_count - 1)
        mask_now = lax.dynamic_index_in_dim(mask_blocks, slot_idx, 0, keepdims=False)
        h_half = run_layer(
            u_half,
            mask_now,
            norm_gains[0],
            q_full[0],
            k_full[0],
            v_full[0],
            out_weights,
            q_rows[0],
            k_rows[0],
            v_rows[0],
            o_rows[0],
        )
        is_valid = (offset >= 0) & (offset < micro_count)
        row_start = slot_idx * seq_len
        current = lax.dynamic_slice_in_dim(results, row_start, seq_len, 0)
        results = lax.dynamic_update_slice_in_dim(
            results, jnp.where(is_valid, h_half, current), row_start, 0
        )
        if step_idx + 1 < total_steps:
            incoming = from_behind(h_half, "pipe", 1)
    return results[None]


def solution(mesh):
    placed = (
        P("fsdp", "tensor"),
        P("pipe", None),
        P("pipe", None, "tensor", "fsdp", None),
        P("pipe", None, "tensor", "fsdp", None),
        P("pipe", None, "tensor", "fsdp", None),
        P("pipe", "tensor", None, "fsdp", None),
        P("pipe", None, "tensor"),
        P("pipe", None, "tensor"),
        P("pipe", None, "tensor"),
        P("pipe", "tensor", None),
        P("fsdp", None, None),
    )
    return jax.shard_map(
        body, mesh=mesh, in_specs=placed, out_specs=P("pipe", "fsdp", "tensor"), check_vma=False
    )
```

profile of v0, /device:TPU:24, one launch (start us, length us, event | category | flops | bytes accessed | tf_op | source)
XLA Modules:
  0.0 689.8 jit_solution(11814978129373047153)
XLA Ops:
  11.5 8.7 %all_gather.30 = bf16[64,4096]{1,0:T(8,128)(2,1)S(1)} all-gather(bf16[64,2048]{1,0:T(8,128)(2,1)S(1)} %slice_select_fusion.2), channel_id=1, replica_groups=mesh['pipe'=4,'fsdp'=32,'tensor'=2] {'tensor'}, dimensions={1}, use_global_device_ids=true | all-gather | bytes 786432 | tf_op jit(solution)/shard_map/all_gather | solution.py:28
  24.7 74.6 %all-gather.7.cloned.1.call-done = bf16[1,4,8,256,256]{4,3,2,1,0:T(8,128)(2,1)} async-done(((bf16[1,4,8,8,256]{4,3,2,1,0:T(8,128)(2,1)}), bf16[1,4,8,256,256]{4,3,2,1,0:T(8,128)(2,1)}) %all-gather.7.cloned.1.call-update) | async-done | bytes 4194320 | tf_op jit(solution)/shard_map/all_gather | solution.py:80
  102.9 82.5 %all-gather.9.cloned.1.call-done = bf16[1,4,8,256,256]{4,3,2,1,0:T(8,128)(2,1)} async-done(((bf16[1,4,8,8,256]{4,3,2,1,0:T(8,128)(2,1)}), bf16[1,4,8,256,256]{4,3,2,1,0:T(8,128)(2,1)}) %all-gather.9.cloned.1.call-update) | async-done | bytes 4194320 | tf_op jit(solution)/shard_map/all_gather | solution.py:81
  188.6 82.8 %all-gather.5.cloned.1.call-done = bf16[1,4,8,256,256]{4,3,2,1,0:T(8,128)(2,1)} async-done(((bf16[1,4,8,8,256]{4,3,2,1,0:T(8,128)(2,1)}), bf16[1,4,8,256,256]{4,3,2,1,0:T(8,128)(2,1)}) %all-gather.5.cloned.1.call-update) | async-done | bytes 4194320 | tf_op jit(solution)/shard_map/all_gather | solution.py:82
  276.3 80.9 %all-gather.11.cloned.1.call-done = bf16[1,2,16,256,256]{4,3,2,1,0:T(8,128)(2,1)} async-done(((bf16[1,2,16,8,256]{4,3,2,1,0:T(8,128)(2,1)}), bf16[1,2,16,256,256]{4,3,2,1,0:T(8,128)(2,1)}) %all-gather.11.cloned.1.call-update) | async-done | bytes 4194320 | tf_op jit(solution)/shard_map/all_gather | solution.py:83
  361.1 16.6 %reduce-scatter.7.cloned.1.call-done = bf16[64,2048]{1,0:T(8,128)(2,1)} async-done(((bf16[64,4096]{1,0:T(8,128)(2,1)}), bf16[64,2048]{1,0:T(8,128)(2,1)}) %reduce-scatter.7.cloned.1.call-update) | async-done | bytes 262160 | tf_op jit(solution)/shard_map/reduce_scatter | solution.py:55
  380.5 8.2 %collective-permute-done = bf16[64,2048]{1,0:T(8,128)(2,1)S(1)} collective-permute-done((bf16[64,2048]{1,0:T(8,128)(2,1)S(1)}, bf16[64,2048]{1,0:T(8,128)(2,1)S(1)}, u32[]{:S(2)}, u32[]{:S(2)}) %collective-permute-start) | collective-permute-done | bytes 262176 | tf_op jit(solution)/shard_map/ppermute | solution.py:13
  389.4 7.7 %all_gather.35 = bf16[64,4096]{1,0:T(8,128)(2,1)S(1)} all-gather(bf16[64,2048]{1,0:T(8,128)(2,1)S(1)} %slice_select_fusion.1), channel_id=1, replica_groups=mesh['pipe'=4,'fsdp'=32,'tensor'=2] {'tensor'}, dimensions={1}, use_global_device_ids=true | all-gather | bytes 786432 | tf_op jit(solution)/shard_map/all_gather | solution.py:28
  400.4 3.3 fusion.261
  417.8 20.8 %reduce-scatter.9.cloned.1.call-done = bf16[64,2048]{1,0:T(8,128)(2,1)} async-done(((bf16[64,4096]{1,0:T(8,128)(2,1)}), bf16[64,2048]{1,0:T(8,128)(2,1)}) %reduce-scatter.9.cloned.1.call-update) | async-done | bytes 262160 | tf_op jit(solution)/shard_map/reduce_scatter | solution.py:55
  441.3 8.2 %collective-permute-done.1 = bf16[64,2048]{1,0:T(8,128)(2,1)S(1)} collective-permute-done((bf16[64,2048]{1,0:T(8,128)(2,1)S(1)}, bf16[64,2048]{1,0:T(8,128)(2,1)S(1)}, u32[]{:S(2)}, u32[]{:S(2)}) %collective-permute-start.1) | collective-permute-done | bytes 262176 | tf_op jit(solution)/shard_map/ppermute | solution.py:13
  451.2 7.9 %all_gather.36 = bf16[64,4096]{1,0:T(8,128)(2,1)S(1)} all-gather(bf16[64,2048]{1,0:T(8,128)(2,1)S(1)} %slice_select_fusion), channel_id=1, replica_groups=mesh['pipe'=4,'fsdp'=32,'tensor'=2] {'tensor'}, dimensions={1}, use_global_device_ids=true | all-gather | bytes 786432 | tf_op jit(solution)/shard_map/all_gather | solution.py:28
  479.8 20.8 %reduce-scatter.11.cloned.1.call-done = bf16[64,2048]{1,0:T(8,128)(2,1)} async-done(((bf16[64,4096]{1,0:T(8,128)(2,1)}), bf16[64,2048]{1,0:T(8,128)(2,1)}) %reduce-scatter.11.cloned.1.call-update) | async-done | bytes 262160 | tf_op jit(solution)/shard_map/reduce_scatter | solution.py:55
  503.2 8.2 %collective-permute-done.2 = bf16[64,2048]{1,0:T(8,128)(2,1)S(1)} collective-permute-done((bf16[64,2048]{1,0:T(8,128)(2,1)S(1)}, bf16[64,2048]{1,0:T(8,128)(2,1)S(1)}, u32[]{:S(2)}, u32[]{:S(2)}) %collective-permute-start.2) | collective-permute-done | bytes 262176 | tf_op jit(solution)/shard_map/ppermute | solution.py:13
  511.5 7.7 %all_gather.37 = bf16[64,4096]{1,0:T(8,128)(2,1)S(1)} all-gather(bf16[64,2048]{1,0:T(8,128)(2,1)S(1)} %broadcast_select_fusion.2), channel_id=1, replica_groups=mesh['pipe'=4,'fsdp'=32,'tensor'=2] {'tensor'}, dimensions={1}, use_global_device_ids=true | all-gather | bytes 786432 | tf_op jit(solution)/shard_map/all_gather | solution.py:28
  522.5 3.3 fusion.267
  539.9 20.8 %reduce-scatter.13.cloned.1.call-done = bf16[64,2048]{1,0:T(8,128)(2,1)} async-done(((bf16[64,4096]{1,0:T(8,128)(2,1)}), bf16[64,2048]{1,0:T(8,128)(2,1)}) %reduce-scatter.13.cloned.1.call-update) | async-done | bytes 262160 | tf_op jit(solution)/shard_map/reduce_scatter | solution.py:55
  563.3 8.2 %collective-permute-done.3 = bf16[64,2048]{1,0:T(8,128)(2,1)S(1)} collective-permute-done((bf16[64,2048]{1,0:T(8,128)(2,1)S(1)}, bf16[64,2048]{1,0:T(8,128)(2,1)S(1)}, u32[]{:S(2)}, u32[]{:S(2)}) %collective-permute-start.3) | collective-permute-done | bytes 262176 | tf_op jit(solution)/shard_map/ppermute | solution.py:13
  571.6 7.9 %all_gather.38 = bf16[64,4096]{1,0:T(8,128)(2,1)S(1)} all-gather(bf16[64,2048]{1,0:T(8,128)(2,1)S(1)} %broadcast_select_fusion.1), channel_id=1, replica_groups=mesh['pipe'=4,'fsdp'=32,'tensor'=2] {'tensor'}, dimensions={1}, use_global_device_ids=true | all-gather | bytes 786432 | tf_op jit(solution)/shard_map/all_gather | solution.py:28
  582.8 3.3 fusion.270
  600.3 20.8 %reduce-scatter.15.cloned.1.call-done = bf16[64,2048]{1,0:T(8,128)(2,1)} async-done(((bf16[64,4096]{1,0:T(8,128)(2,1)}), bf16[64,2048]{1,0:T(8,128)(2,1)}) %reduce-scatter.15.cloned.1.call-update) | async-done | bytes 262160 | tf_op jit(solution)/shard_map/reduce_scatter | solution.py:55
  623.7 8.2 %collective-permute-done.4 = bf16[64,2048]{1,0:T(8,128)(2,1)S(1)} collective-permute-done((bf16[64,2048]{1,0:T(8,128)(2,1)S(1)}, bf16[64,2048]{1,0:T(8,128)(2,1)S(1)}, u32[]{:S(2)}, u32[]{:S(2)}) %collective-permute-start.4) | collective-permute-done | bytes 262176 | tf_op jit(solution)/shard_map/ppermute | solution.py:13
  631.9 7.7 %all_gather.39 = bf16[64,4096]{1,0:T(8,128)(2,1)S(1)} all-gather(bf16[64,2048]{1,0:T(8,128)(2,1)S(1)} %broadcast_select_fusion), channel_id=1, replica_groups=mesh['pipe'=4,'fsdp'=32,'tensor'=2] {'tensor'}, dimensions={1}, use_global_device_ids=true | all-gather | bytes 786432 | tf_op jit(solution)/shard_map/all_gather | solution.py:28
  661.2 20.0 %reduce-scatter.17.cloned.1.call-done = bf16[64,2048]{1,0:T(8,128)(2,1)} async-done(((bf16[64,4096]{1,0:T(8,128)(2,1)}), bf16[64,2048]{1,0:T(8,128)(2,1)}) %reduce-scatter.17.cloned.1.call-update) | async-done | bytes 262160 | tf_op jit(solution)/shard_map/reduce_scatter | solution.py:55
  (254 shorter events, 136.0 us)
Async XLA Ops:
  6.5 14.9 %copy-start.13 = (s32[1,4,8]{2,1,0:T(4,128)S(1)}, s32[1,4,8]{2,1,0:T(4,128)}, u32[]{:S(2)}) copy-start(s32[1,4,8]{2,1,0:T(4,128)} %param.18) | copy-start | bytes 388
  6.5 92.7 %all-gather.7.cloned.1.call-start = ((), (), s32[]{:S(2)}) async-start(), calls=%async_computation.7 | async-start | bytes 4325376 | tf_op jit(solution)/shard_map/all_gather | solution.py:80
  7.3 178.1 %all-gather.9.cloned.1.call-start = ((), (), s32[]{:S(2)}) async-start(), calls=%async_computation.8 | async-start | bytes 4325376 | tf_op jit(solution)/shard_map/all_gather | solution.py:81
  8.0 263.3 %all-gather.5.cloned.1.call-start = ((), (), s32[]{:S(2)}) async-start(), calls=%async_computation.6 | async-start | bytes 4325376 | tf_op jit(solution)/shard_map/all_gather | solution.py:82
  8.7 15.1 %copy-start.12 = (s32[1,4,8]{2,1,0:T(4,128)S(1)}, s32[1,4,8]{2,1,0:T(4,128)}, u32[]{:S(2)}) copy-start(s32[1,4,8]{2,1,0:T(4,128)} %param.19) | copy-start | bytes 388
  8.8 348.5 %all-gather.11.cloned.1.call-start = ((), (), s32[]{:S(2)}) async-start(), calls=%async_computation.9 | async-start | bytes 4325376 | tf_op jit(solution)/shard_map/all_gather | solution.py:83
  9.3 368.4 %reduce-scatter.7.cloned.1.call-start = ((), (), s32[]{:S(2)}) async-start(), calls=%async_computation.10 | async-start | bytes 786432 | tf_op jit(solution)/shard_map/reduce_scatter | solution.py:55
  276.3 101.5 %copy-start.4 = (bf16[192,2048]{1,0:T(8,128)(2,1)S(1)}, bf16[192,2048]{1,0:T(8,128)(2,1)}, u32[]{:S(2)}) copy-start(bf16[192,2048]{1,0:T(8,128)(2,1)} %param.11) | copy-start | bytes 2359300
  360.2 37.1 %copy-start.11 = (f32[1,4096]{1,0:T(1,128)S(1)}, f32[1,4096]{1,0:T(1,128)}, u32[]{:S(2)}) copy-start(f32[1,4096]{1,0:T(1,128)} %param.12) | copy-start | bytes 49156
  361.1 77.5 %reduce-scatter.9.cloned.1.call-start = ((), (), s32[]{:S(2)}) async-start(), calls=%async_computation.11 | async-start | bytes 786432 | tf_op jit(solution)/shard_map/reduce_scatter | solution.py:55
  378.9 9.8 %collective-permute-start = (bf16[64,2048]{1,0:T(8,128)(2,1)S(1)}, bf16[64,2048]{1,0:T(8,128)(2,1)S(1)}, u32[]{:S(2)}, u32[]{:S(2)}) collective-permute-start(bf16[64,2048]{1,0:T(8,128)(2,1)S(1)} %get-tuple-element.14), channel_id=1, source_target_pairs={{0,64},{64,128},{128,192},{1,65},{65,129},{129,193},{2,66},{66,130... | collective-permute-start | bytes 786440 | tf_op jit(solution)/shard_map/ppermute | solution.py:13
  413.9 24.7 %copy-start.1 = (bf16[64,2048]{1,0:T(8,128)(2,1)S(1)}, bf16[64,2048]{1,0:T(8,128)(2,1)}, u32[]{:S(2)}) copy-start(bf16[64,2048]{1,0:T(8,128)(2,1)} %copy-done) | copy-start | bytes 786436
  417.8 82.8 %reduce-scatter.11.cloned.1.call-start = ((), (), s32[]{:S(2)}) async-start(), calls=%async_computation.12 | async-start | bytes 786432 | tf_op jit(solution)/shard_map/reduce_scatter | solution.py:55
  439.7 9.8 %collective-permute-start.1 = (bf16[64,2048]{1,0:T(8,128)(2,1)S(1)}, bf16[64,2048]{1,0:T(8,128)(2,1)S(1)}, u32[]{:S(2)}, u32[]{:S(2)}) collective-permute-start(bf16[64,2048]{1,0:T(8,128)(2,1)S(1)} %get-tuple-element.12), channel_id=1, source_target_pairs={{0,64},{64,128},{128,192},{1,65},{65,129},{129,193},{2,66},{66,130... | collective-permute-start | bytes 786440 | tf_op jit(solution)/shard_map/ppermute | solution.py:13
  475.8 24.8 %copy-start.3 = (bf16[64,2048]{1,0:T(8,128)(2,1)S(1)}, bf16[64,2048]{1,0:T(8,128)(2,1)}, u32[]{:S(2)}) copy-start(bf16[64,2048]{1,0:T(8,128)(2,1)} %copy-done.2) | copy-start | bytes 786436
  479.7 81.0 %reduce-scatter.13.cloned.1.call-start = ((), (), s32[]{:S(2)}) async-start(), calls=%async_computation.13 | async-start | bytes 786432 | tf_op jit(solution)/shard_map/reduce_scatter | solution.py:55
  501.7 9.8 %collective-permute-start.2 = (bf16[64,2048]{1,0:T(8,128)(2,1)S(1)}, bf16[64,2048]{1,0:T(8,128)(2,1)S(1)}, u32[]{:S(2)}, u32[]{:S(2)}) collective-permute-start(bf16[64,2048]{1,0:T(8,128)(2,1)S(1)} %get-tuple-element.10), channel_id=1, source_target_pairs={{0,64},{64,128},{128,192},{1,65},{65,129},{129,193},{2,66},{66,130... | collective-permute-start | bytes 786440 | tf_op jit(solution)/shard_map/ppermute | solution.py:13
  535.9 24.7 %copy-start.8 = (bf16[64,2048]{1,0:T(8,128)(2,1)S(1)}, bf16[64,2048]{1,0:T(8,128)(2,1)}, u32[]{:S(2)}) copy-start(bf16[64,2048]{1,0:T(8,128)(2,1)} %copy-done.7) | copy-start | bytes 786436
  539.8 81.2 %reduce-scatter.15.cloned.1.call-start = ((), (), s32[]{:S(2)}) async-start(), calls=%async_computation.14 | async-start | bytes 786432 | tf_op jit(solution)/shard_map/reduce_scatter | solution.py:55
  561.8 9.8 %collective-permute-start.3 = (bf16[64,2048]{1,0:T(8,128)(2,1)S(1)}, bf16[64,2048]{1,0:T(8,128)(2,1)S(1)}, u32[]{:S(2)}, u32[]{:S(2)}) collective-permute-start(bf16[64,2048]{1,0:T(8,128)(2,1)S(1)} %get-tuple-element.8), channel_id=1, source_target_pairs={{0,64},{64,128},{128,192},{1,65},{65,129},{129,193},{2,66},{66,130... | collective-permute-start | bytes 786440 | tf_op jit(solution)/shard_map/ppermute | solution.py:13
  596.3 24.7 %copy-start.10 = (bf16[64,2048]{1,0:T(8,128)(2,1)S(1)}, bf16[64,2048]{1,0:T(8,128)(2,1)}, u32[]{:S(2)}) copy-start(bf16[64,2048]{1,0:T(8,128)(2,1)} %copy-done.9) | copy-start | bytes 786436
  600.2 81.0 %reduce-scatter.17.cloned.1.call-start = ((), (), s32[]{:S(2)}) async-start(), calls=%async_computation.15 | async-start | bytes 786432 | tf_op jit(solution)/shard_map/reduce_scatter | solution.py:55
  622.1 9.8 %collective-permute-start.4 = (bf16[64,2048]{1,0:T(8,128)(2,1)S(1)}, bf16[64,2048]{1,0:T(8,128)(2,1)S(1)}, u32[]{:S(2)}, u32[]{:S(2)}) collective-permute-start(bf16[64,2048]{1,0:T(8,128)(2,1)S(1)} %get-tuple-element.6), channel_id=1, source_target_pairs={{0,64},{64,128},{128,192},{1,65},{65,129},{129,193},{2,66},{66,130... | collective-permute-start | bytes 786440 | tf_op jit(solution)/shard_map/ppermute | solution.py:13
  656.4 24.7 %copy-start.6 = (bf16[64,2048]{1,0:T(8,128)(2,1)S(1)}, bf16[64,2048]{1,0:T(8,128)(2,1)}, u32[]{:S(2)}) copy-start(bf16[64,2048]{1,0:T(8,128)(2,1)} %copy-done.5) | copy-start | bytes 786436
  (7 other events, 45.1 us)
Sparse Core Ops, SparseCore 0:
  9.9 89.3 all-gather.6
  101.8 83.4 all-gather.8
  187.9 83.4 all-gather.4
  273.8 83.4 all-gather.10
  361.2 16.4 reduce-scatter.6
  417.9 20.6 reduce-scatter.8
  479.8 20.7 reduce-scatter.10
  539.9 20.6 reduce-scatter.12
  600.3 20.6 reduce-scatter.14
  660.4 20.6 reduce-scatter.16
where the time goes:
time: 692 us; the launch traced here: 690 us
  waiting for transfers between devices  484 us (70%)
  matrix products  82.2 us (12%)
  blocking collectives  47.5 us (7%)
  local copies, waits for them, and re-layouts  40.1 us (6%)
  between operations  14.9 us (2%)
  other arithmetic  14.1 us (2%)
    reduce_scatter x6, waiting for transfers between devices, run_layer(): lax.psum_scatter(partial_out.astype(jnp.bfloat16), 'tensor', scatter_dime...  120 us
    all_gather x1, waiting for transfers between devices, body(): lax.all_gather(v_blocks, 'fsdp', axis=3, tiled=True)  82.8 us
    all_gather x1, waiting for transfers between devices, body(): lax.all_gather(k_blocks, 'fsdp', axis=3, tiled=True)  82.5 us
    all_gather x1, waiting for transfers between devices, body(): lax.all_gather(o_blocks, 'fsdp', axis=3, tiled=True)  80.9 us
    all_gather x1, waiting for transfers between devices, body(): lax.all_gather(q_blocks, 'fsdp', axis=3, tiled=True)  74.6 us
    dot_general x24, matrix products, block_project(): jnp.einsum('rpcb,pcbe->rce', picked, blocks, preferred_element_type=jnp.f...  73.8 us
    all_gather x6, blocking collectives, run_layer(): gathered = lax.all_gather(u_half, 'tensor', axis=1, tiled=True)  47.5 us
    ppermute x5, waiting for transfers between devices, from_behind(): lax.ppermute(value, axis, [(source, source + steps) for source in range(i...  41 us
  transfers between devices with their start and end apart: 15, of which 15 were waited for; matrix products, arithmetic and copies ran while one was open for 3% of the time, Pallas kernels for 0%

commit v1 on v0

v1 whole, which is shorter than its diff:
```python
import functools

import jax
import jax.numpy as jnp
from jax import lax
from jax.experimental import pallas as pl
from jax.experimental.pallas import tpu as pltpu
from jax.sharding import PartitionSpec as P

HD = 128
MBLK = 16
MESH = pl.DeviceIdType.MESH
MATS = 4
BS = 256
UNIT = 16
LATE = (3,)


def kernel(
    sizes, tok, gain, q, k, v, o, q_rows, k_rows, v_rows, o_rows, mask, out,
    weights, raw, u_buf, normed, att, own, rs_send, rs_recv,
    cx_send, cx_recv, xe_send, xe_recv, xl_send, xl_recv, z_send, z_recv, cf_send, cf_recv,
    tk_send, tk_recv, rs_ssem, rs_rsem, u_ssem, u_rsem,
):
    nz, samples, seq = sizes
    pipe = lax.axis_index("pipe")
    fsdp = lax.axis_index("fsdp")
    t = lax.axis_index("tensor")
    pipes = lax.axis_size("pipe")
    core = lax.rem(fsdp, 2)
    z = lax.rem(fsdp // 2, nz)
    h = fsdp // (2 * nz)
    mate = fsdp + 1 - 2 * core

    def at_fsdp(hh, zz):
        return (hh * nz + zz) * 2 + core

    across = at_fsdp(1 - h, z)
    up = at_fsdp(h, lax.rem(z + 1, nz))
    down = at_fsdp(h, lax.rem(z + nz - 1, nz))
    previous = lax.rem(pipe + pipes - 1, pipes)

    barrier = pltpu.get_barrier_semaphore()
    for target in (mate, across, up, down):
        pl.semaphore_signal(barrier, inc=1, device_id={"fsdp": target}, device_id_type=MESH)
    pl.semaphore_signal(barrier, inc=1, device_id={"tensor": 1 - t}, device_id_type=MESH)
    for other in (t, 1 - t):
        pl.semaphore_signal(
            barrier, inc=1, device_id={"pipe": previous, "tensor": other}, device_id_type=MESH
        )
    pl.semaphore_wait(barrier, 7)

    shards = (q, k, v, o)
    halves = shards[0].shape[0] // 2
    mine = pl.ds(core * halves, halves)
    theirs = pl.ds((1 - core) * halves, halves)

    def remote(src, dst, ssem, rsem, device):
        return pltpu.make_async_remote_copy(
            src_ref=src, dst_ref=dst, send_sem=ssem, recv_sem=rsem, device_id=device,
            device_id_type=MESH,
        )

    swaps = []
    for mat in range(MATS):
        copy = remote(
            shards[mat].at[theirs], raw.at[mat], cx_send.at[mat], cx_recv.at[mat], {"fsdp": mate}
        )
        copy.start()
        swaps.append(copy)

    half_blocks = tok.shape[1] // BS

    def token_copy(b):
        return remote(
            tok.at[:, pl.ds(b * BS, BS)], u_buf.at[t * half_blocks + b], tk_send.at[b],
            tk_recv.at[b], {"tensor": 1 - t},
        )

    @pl.when(pipe == 0)
    def _():
        for b in range(half_blocks):
            token_copy(b).start()
        for b in range(half_blocks):
            u_buf[t * half_blocks + b] = tok[:, b * BS : (b + 1) * BS]

    def rows_of(hh, zz):
        return pl.ds(pl.multiple_of((hh * nz + zz) * UNIT, UNIT), UNIT)

    def piece(mat, hh, zz):
        return weights.at[mat, mine, rows_of(hh, zz)]

    def z_copy(way, slot, mat, step, hh, zz):
        target = up if way == 0 else down
        return remote(
            piece(mat, hh, zz), piece(mat, hh, zz), z_send.at[way, mat],
            z_recv.at[way, slot, mat, step], {"fsdp": target},
        )

    def core_copy(mat, hh, zz):
        return remote(
            piece(mat, hh, zz), piece(mat, hh, zz), cf_send.at[mat], cf_recv.at[mat],
            {"fsdp": mate},
        )

    def early_copy(mat):
        return remote(
            piece(mat, h, z), piece(mat, h, z), xe_send.at[mat], xe_recv.at[mat],
            {"fsdp": across},
        )

    def late_copy(mat, slot, hh, zz):
        return remote(
            piece(mat, hh, zz), piece(mat, hh, zz), xl_send.at[mat], xl_recv.at[mat, slot],
            {"fsdp": across},
        )

    def steps_of(way, mat):
        long = nz // 2
        return long if (mat % 2 == way) else nz - 1 - long

    for mat in range(MATS):
        swaps[mat].wait_recv()

        def join(i, carry, mat=mat):
            low = shards[mat][core * halves + i]
            high = raw[mat, i]
            first = jnp.where(core == 0, low, high)
            second = jnp.where(core == 0, high, low)
            weights[mat, core * halves + i, rows_of(h, z), :] = jnp.concatenate(
                [first, second], axis=0
            )
            return carry

        lax.fori_loop(0, halves, join, 0)
        if mat not in LATE:
            early_copy(mat).start()
        for way in range(2):
            z_copy(way, 0, mat, 0, h, z).start()
        core_copy(mat, h, z).start()
        if mat in LATE:
            late_copy(mat, 0, h, z).start()
    for mat in range(MATS):
        if mat in LATE:
            continue
        pltpu.make_async_copy(piece(mat, 1 - h, z), piece(mat, 1 - h, z), xe_recv.at[mat]).wait()
        for way in range(2):
            z_copy(way, 1, mat, 0, 1 - h, z).start()
        core_copy(mat, 1 - h, z).start()

    def got(ref, sem):
        pltpu.make_async_copy(ref, ref, sem).wait()

    late_queue = [(mat, 0, z) for mat in LATE]

    def drain_late(entries):
        for mat, slot, zz in entries:
            got(piece(mat, 1 - h, zz), xl_recv.at[mat, slot])
            core_copy(mat, 1 - h, zz).start()

    for step in range(nz // 2):
        pending, late_queue = late_queue, []
        for mat in range(MATS):
            for slot in range(1 if mat in LATE else 2):
                hh = h if slot == 0 else 1 - h
                for way in range(2):
                    if step >= steps_of(way, mat):
                        continue
                    if way == 0:
                        zz = lax.rem(z + nz - step - 1, nz)
                    else:
                        zz = lax.rem(z + step + 1, nz)
                    got(piece(mat, hh, zz), z_recv.at[way, slot, mat, step])
                    if step + 1 < steps_of(way, mat):
                        z_copy(way, slot, mat, step + 1, hh, zz).start()
                    core_copy(mat, hh, zz).start()
                    if mat in LATE:
                        place = 1 + step + way * steps_of(0, mat)
                        late_copy(mat, place, hh, zz).start()
                        late_queue.append((mat, place, zz))
        drain_late(pending)
    drain_late(late_queue)

    full = weights.shape[2]
    for mat in range(MATS):
        got(weights.at[mat, theirs], cf_recv.at[mat])

    @pl.when(pipe == 0)
    def _():
        for b in range(half_blocks):
            token_copy(b).wait()

    lanes = lax.broadcasted_iota(jnp.int32, (seq, seq), 1) // MBLK
    sublanes = lax.broadcasted_iota(jnp.int32, (seq, seq), 0) // MBLK
    mask_blocks = seq // MBLK
    all_blocks = 2 * half_blocks
    per = q_rows.shape[0]
    columns = q_rows.shape[1]
    chunks = 2
    chunk = half_blocks // chunks
    nt = (((1,), (1,)), ((), ()))

    def rs_copy(m, j, rows):
        where = pl.ds(j * chunk, chunk)
        return remote(
            rs_send.at[where, rows], rs_recv.at[where, rows], rs_ssem.at[m, j], rs_rsem.at[m, j],
            {"tensor": 1 - t},
        )

    def u_copy(m, j, rows, side):
        target = t if side == 0 else 1 - t
        return remote(
            out.at[pl.ds(j * chunk, chunk), rows],
            u_buf.at[pl.ds(t * half_blocks + j * chunk, chunk), rows],
            u_ssem.at[m, j, side], u_rsem.at[m, j, side],
            {"pipe": lax.rem(pipe + 1, pipes), "tensor": target},
        )

    def sample(m, carry):
        rows = pl.ds(pl.multiple_of(m * seq, seq), seq)

        @pl.when(pipe > 0)
        def _():
            for j in range(chunks):
                for side in range(2):
                    source = t if side == 0 else 1 - t
                    got(
                        u_buf.at[pl.ds(source * half_blocks + j * chunk, chunk), rows],
                        u_rsem.at[m, j, side],
                    )

        total = jnp.zeros((seq, BS), jnp.float32)
        for b in range(all_blocks):
            values = u_buf[b, rows, :].astype(jnp.float32)
            total = total + values * values
        mean = jnp.sum(total, axis=-1, keepdims=True) * (1.0 / (all_blocks * BS))
        inv_rms = lax.rsqrt(mean + 1e-05)
        for b in range(all_blocks):
            values = u_buf[b, rows, :].astype(jnp.float32)
            normed[b] = (values * inv_rms * gain[:, b * BS : (b + 1) * BS]).astype(jnp.bfloat16)

        allowed = jnp.zeros((seq, seq), jnp.int32)
        for i in range(mask_blocks):
            for jj in range(mask_blocks):
                here = (sublanes == i) & (lanes == jj)
                allowed = jnp.where(here, mask[m, i, jj], allowed)

        def project(mat, table, c):
            acc = None
            for p in range(per):
                term = jnp.dot(
                    normed[table[p, c]], weights[mat, p * columns + c],
                    preferred_element_type=jnp.float32,
                )
                acc = term if acc is None else acc + term
            return acc.astype(jnp.bfloat16)

        def column(c, inner):
            queries = project(0, q_rows, c)
            keys = project(1, k_rows, c)
            values = project(2, v_rows, c)
            for head in range(BS // HD):
                cut = slice(head * HD, (head + 1) * HD)
                scores = lax.dot_general(
                    queries[:, cut], keys[:, cut], nt, preferred_element_type=jnp.float32
                ) * HD ** (-0.5)
                scores = jnp.where(allowed == 1, scores, jnp.float32(-1e30))
                top = jnp.max(scores, axis=-1, keepdims=True)
                exps = jnp.exp(scores - top)
                probs = (exps / jnp.sum(exps, axis=-1, keepdims=True)).astype(jnp.bfloat16)
                att[c, :, cut] = jnp.dot(
                    probs, values[:, cut], preferred_element_type=jnp.float32
                ).astype(jnp.bfloat16)
            return inner

        lax.fori_loop(0, columns, column, 0, unroll=2)

        picks = o_rows.shape[0]

        def out_column(c):
            acc = None
            for p in range(picks):
                term = jnp.dot(
                    att[o_rows[p, c]], weights[3, p * all_blocks + c],
                    preferred_element_type=jnp.float32,
                )
                acc = term if acc is None else acc + term
            return acc

        for j in range(chunks):
            def away(i, inner):
                rs_send[i, rows, :] = out_column((1 - t) * half_blocks + i).astype(jnp.bfloat16)
                return inner

            lax.fori_loop(j * chunk, (j + 1) * chunk, away, 0, unroll=4)
            rs_copy(m, j, rows).start()

        def home(i, inner):
            own[i] = out_column(t * half_blocks + i)
            return inner

        lax.fori_loop(0, half_blocks, home, 0, unroll=4)
        for j in range(chunks):
            rs_copy(m, j, rows).wait_recv()
            for i in range(j * chunk, (j + 1) * chunk):
                base = u_buf[t * half_blocks + i, rows, :].astype(jnp.float32)
                branch = own[i] + rs_recv[i, rows, :].astype(jnp.float32)
                out[i, rows, :] = (base + branch).astype(jnp.bfloat16)

            @pl.when(pipe < pipes - 1)
            def _(j=j):
                for side in range(2):
                    u_copy(m, j, rows, side).start()

        return carry

    lax.fori_loop(0, samples, sample, 0)

    def drain(m, carry):
        rows = pl.ds(pl.multiple_of(m * seq, seq), seq)
        for j in range(chunks):
            rs_copy(m, j, rows).wait_send()

            @pl.when(pipe < pipes - 1)
            def _(j=j):
                for side in range(2):
                    u_copy(m, j, rows, side).wait_send()

        return carry

    lax.fori_loop(0, samples, drain, 0)
    for mat in range(MATS):
        swaps[mat].wait_send()
        got(weights.at[mat, mine], cf_send.at[mat])
        count = 1 if mat in LATE else 2
        for way in range(2):
            got(
                weights.at[mat, mine, pl.ds(0, UNIT * count * steps_of(way, mat))],
                z_send.at[way, mat],
            )
        if mat in LATE:
            got(weights.at[mat, mine, pl.ds(0, UNIT * nz)], xl_send.at[mat])
        else:
            got(piece(mat, h, z), xe_send.at[mat])


def body(
    tokens, norm_gains, q_blocks, k_blocks, v_blocks, o_blocks, q_rows, k_rows, v_rows, o_rows,
    mask_blocks,
):
    samples = mask_blocks.shape[0]
    row_count, half_width = tokens.shape
    seq = row_count // samples
    half = half_width // BS
    nz = lax.axis_size("fsdp") // 4
    shards = [
        w.reshape(-1, w.shape[-2], w.shape[-1]) for w in (q_blocks, k_blocks, v_blocks, o_blocks)
    ]
    blocks, depth, _ = shards[0].shape
    vmem = pl.BlockSpec(memory_space=pltpu.VMEM)
    smem = pl.BlockSpec(memory_space=pltpu.SMEM)
    dma = pltpu.SemaphoreType.DMA
    result = pl.pallas_call(
        functools.partial(kernel, (nz, samples, seq)),
        out_shape=jax.ShapeDtypeStruct((half, row_count, BS), jnp.bfloat16),
        in_specs=[vmem] * 6 + [smem] * 5,
        out_specs=vmem,
        scratch_shapes=[
            pltpu.VMEM((MATS, blocks, BS, BS), jnp.bfloat16),
            pltpu.VMEM((MATS, blocks // 2, depth, BS), jnp.bfloat16),
            pltpu.VMEM((2 * half, row_count, BS), jnp.bfloat16),
            pltpu.VMEM((2 * half, seq, BS), jnp.bfloat16),
            pltpu.VMEM((half, seq, BS), jnp.bfloat16),
            pltpu.VMEM((half, seq, BS), jnp.float32),
            pltpu.VMEM((half, row_count, BS), jnp.bfloat16),
            pltpu.VMEM((half, row_count, BS), jnp.bfloat16),
            dma((MATS,)),
            dma((MATS,)),
            dma((MATS,)),
            dma((MATS,)),
            dma((MATS,)),
            dma((MATS, nz)),
            dma((2, MATS)),
            dma((2, 2, MATS, nz // 2)),
            dma((MATS,)),
            dma((MATS,)),
            dma((half,)),
            dma((half,)),
            dma((samples, 2)),
            dma((samples, 2)),
            dma((samples, 2, 2)),
            dma((samples, 2, 2)),
        ],
        compiler_params=pltpu.CompilerParams(
            collective_id=0, has_side_effects=True, vmem_limit_bytes=48 << 20
        ),
    )(
        tokens, norm_gains, *shards, q_rows[0], k_rows[0], v_rows[0], o_rows[0], mask_blocks
    )
    return jnp.transpose(result, (1, 0, 2)).reshape(1, row_count, half_width)


def solution(mesh):
    placed = (
        P("fsdp", "tensor"),
        P("pipe", None),
        P("pipe", None, "tensor", "fsdp", None),
        P("pipe", None, "tensor", "fsdp", None),
        P("pipe", None, "tensor", "fsdp", None),
        P("pipe", "tensor", None, "fsdp", None),
        P("pipe", None, "tensor"),
        P("pipe", None, "tensor"),
        P("pipe", None, "tensor"),
        P("pipe", "tensor", None),
        P("fsdp", None, None),
    )
    return jax.shard_map(
        body, mesh=mesh, in_specs=placed, out_specs=P("pipe", "fsdp", "tensor"), check_vma=False
    )
```

time: 692 us -> 225 us (0.33)
  waiting for transfers between devices: 484 us -> 0 us
  Pallas kernels: 0 us -> 216 us
  matrix products: 82.2 us -> 0 us
  blocking collectives: 47.5 us -> 0 us
  local copies, waits for them, and re-layouts: 40.1 us -> 7.86 us
  between operations: 14.9 us -> 0.04 us
  other arithmetic: 14.1 us -> 0 us
    all_gather x4 -> x0, waiting for transfers between devices: 321 us -> none  [the longest x1 82.8 us: body(): lax.all_gather(v_blocks, 'fsdp', axis=3, tiled=True)]
    pallas_call x0 -> x1, Pallas kernels: none -> 216 us  [body(): pl.pallas_call(functools.partial(kernel, (nz, samples, seq)), out_shape=j...]
    reduce_scatter x6 -> x0, waiting for transfers between devices: 120 us -> none  [run_layer(): lax.psum_scatter(partial_out.astype(jnp.bfloat16), 'tensor', scatter_dime...]
    dot_general x36 -> x0, matrix products: 82.2 us -> none  [the longest x24 73.8 us: block_project(): jnp.einsum('rpcb,pcbe->rce', picked, blocks, preferred_element_type=jnp.f...]
    all_gather x6 -> x0, blocking collectives: 47.5 us -> none  [run_layer(): gathered = lax.all_gather(u_half, 'tensor', axis=1, tiled=True)]
    ppermute x5 -> x0, waiting for transfers between devices: 41 us -> none  [from_behind(): lax.ppermute(value, axis, [(source, source + steps) for source in range(i...]
    gather x24 -> x0, local copies, waits for them, and re-layouts: 20.7 us -> none  [block_project(): picked = row_blocks[:, pattern]]
    convert_element_type x48 -> x0, local copies, waits for them, and re-layouts: 13.9 us -> none  [the longest x6 4.96 us: run_layer(): partial_out.astype(jnp.bfloat16)]
  transfers between devices with their start and end apart: 15 -> 0, of which waited for: 15 -> 0; matrix products, arithmetic and copies ran while one was open for 3% -> 0% of each run, Pallas kernels for 0% -> 0%
where the time goes in v1:
time: 225 us; the launch traced here: 224 us
  Pallas kernels  216 us (96%)
  local copies, waits for them, and re-layouts  7.86 us (3%)
    pallas_call x1, Pallas kernels, body(): pl.pallas_call(functools.partial(kernel, (nz, samples, seq)), out_shape=j...  216 us
    unnamed x22, local copies, waits for them, and re-layouts  6.18 us

profile of v1, /device:TPU:24, one launch (start us, length us, event | category | flops | bytes accessed | tf_op | source)
XLA Modules:
  0.0 224.3 jit_solution(10210323669080120498)
XLA Ops:
  0.0 0.0 copy-start.9
  0.0 0.0 copy-start.8
  0.0 0.0 copy-start.7
  0.0 0.0 copy-start.10
  0.0 0.7 copy-done.9
  0.7 0.0 copy-done.6
  0.7 0.0 copy-done.8
  0.7 0.0 copy-done.7
  0.7 0.0 copy-done.10
  0.7 0.0 copy-start
  0.7 1.1 copy-done
  1.9 0.0 copy-start.1
  1.9 0.9 copy-done.1
  2.8 0.0 copy-start.2
  2.8 0.9 copy-done.2
  3.7 0.0 copy-start.3
  3.7 0.9 copy-done.3
  4.6 0.0 copy-start.4
  4.6 0.9 copy-done.4
  5.5 0.0 copy-start.5
  5.5 0.7 copy-done.5
  6.2 216.4 %shard_map.109 = bf16[8,192,256]{2,1,0:T(8,128)(2,1)S(1)} custom-call(bf16[192,2048]{1,0:T(8,128)(2,1)S(1)} %copy-done, f32[1,4096]{1,0:T(1,128)S(1)} %copy-done.5, bf16[32,8,256]{2,1,0:T(8,128)(2,1)S(1)} %bitcast.10, bf16[32,8,256]{2,1,0:T(8,128)(2,1)S(1)} %bitcast.11, bf16[32,8,256]{2,1,0:T(8,128)(2,1)S(1)} %bitcast.12, bf16[32,8,256]{2,1,0:T(8,128)(2,1)S(1)} %bitcast.13, ...), custom_call_target="tpu_custom_call" | custom-call | tf_op jit(solution)/shard_map/pallas_call | solution.py:363
  222.6 0.4 copy.12
  223.1 1.2 reshape.19
  (1 shorter events, 0.0 us)
Async XLA Ops:
  0.0 0.7 copy-start.9
  0.0 0.7 copy-start.6
  0.0 0.7 copy-start.8
  0.0 0.7 copy-start.7
  0.0 0.7 copy-start.10
  0.7 1.1 copy-start
  1.9 0.9 copy-start.1
  2.8 0.9 copy-start.2
  3.7 0.9 copy-start.3
  4.6 0.9 copy-start.4
  5.5 0.7 copy-start.5

commit v2 on v1

--- a/solution.py
+++ b/solution.py
@@ -13,14 +13,16 @@
 MATS = 4
 BS = 256
 UNIT = 16
-LATE = (3,)
+LATE = (0, 1)
+UNROLL_P = 2
+UNROLL_A = 4
 
 
 def kernel(
     sizes, tok, gain, q, k, v, o, q_rows, k_rows, v_rows, o_rows, mask, out,
-    weights, raw, u_buf, normed, att, own, rs_send, rs_recv,
+    weights, raw, near, u_buf, normed, heads, att, own, rs_send, rs_recv, near_sem,
     cx_send, cx_recv, xe_send, xe_recv, xl_send, xl_recv, z_send, z_recv, cf_send, cf_recv,
-    tk_send, tk_recv, rs_ssem, rs_rsem, u_ssem, u_rsem,
+    tk_send, tk_recv, own_sem, rs_ssem, rs_rsem, u_ssem, u_rsem,
 ):
     nz, samples, seq = sizes
     pipe = lax.axis_index("pipe")
@@ -68,21 +70,30 @@
         )
         copy.start()
         swaps.append(copy)
+        pltpu.make_async_copy(shards[mat].at[mine], near.at[mat], near_sem.at[mat]).start()
 
     half_blocks = tok.shape[1] // BS
 
-    def token_copy(b):
-        return remote(
-            tok.at[:, pl.ds(b * BS, BS)], u_buf.at[t * half_blocks + b], tk_send.at[b],
-            tk_recv.at[b], {"tensor": 1 - t},
-        )
-
-    @pl.when(pipe == 0)
-    def _():
-        for b in range(half_blocks):
-            token_copy(b).start()
-        for b in range(half_blocks):
-            u_buf[t * half_blocks + b] = tok[:, b * BS : (b + 1) * BS]
+    def sample_rows(m):
+        return pl.ds(pl.multiple_of(m * seq, seq), seq)
+
+    def token_copy(m, b):
+        return remote(
+            tok.at[sample_rows(m), pl.ds(b * BS, BS)], u_buf.at[t * half_blocks + b, sample_rows(m)],
+            tk_send.at[m], tk_recv.at[m], {"tensor": 1 - t},
+        )
+
+    def token_local(b):
+        return pltpu.make_async_copy(
+            tok.at[:, pl.ds(b * BS, BS)], u_buf.at[t * half_blocks + b], own_sem.at[b]
+        )
+
+    def send_tokens(first, last):
+        @pl.when(pipe == 0)
+        def _():
+            for m in range(first, last):
+                for b in range(half_blocks):
+                    token_copy(m, b).start()
 
     def rows_of(hh, zz):
         return pl.ds(pl.multiple_of((hh * nz + zz) * UNIT, UNIT), UNIT)
@@ -121,9 +132,10 @@
 
     for mat in range(MATS):
         swaps[mat].wait_recv()
+        pltpu.make_async_copy(shards[mat].at[mine], near.at[mat], near_sem.at[mat]).wait()
 
         def join(i, carry, mat=mat):
-            low = shards[mat][core * halves + i]
+            low = near[mat, i]
             high = raw[mat, i]
             first = jnp.where(core == 0, low, high)
             second = jnp.where(core == 0, high, low)
@@ -132,7 +144,7 @@
             )
             return carry
 
-        lax.fori_loop(0, halves, join, 0)
+        lax.fori_loop(0, halves, join, 0, unroll=4)
         if mat not in LATE:
             early_copy(mat).start()
         for way in range(2):
@@ -140,6 +152,13 @@
         core_copy(mat, h, z).start()
         if mat in LATE:
             late_copy(mat, 0, h, z).start()
+    send_tokens(0, 1)
+
+    @pl.when(pipe == 0)
+    def _():
+        for b in range(half_blocks):
+            token_local(b).start()
+
     for mat in range(MATS):
         if mat in LATE:
             continue
@@ -179,6 +198,7 @@
                         late_copy(mat, place, hh, zz).start()
                         late_queue.append((mat, place, zz))
         drain_late(pending)
+    send_tokens(1, samples)
     drain_late(late_queue)
 
     full = weights.shape[2]
@@ -188,10 +208,11 @@
     @pl.when(pipe == 0)
     def _():
         for b in range(half_blocks):
-            token_copy(b).wait()
-
-    lanes = lax.broadcasted_iota(jnp.int32, (seq, seq), 1) // MBLK
-    sublanes = lax.broadcasted_iota(jnp.int32, (seq, seq), 0) // MBLK
+            token_local(b).wait()
+
+    pair = BS // HD
+    query_block = lax.rem(lax.broadcasted_iota(jnp.int32, (seq, pair * seq), 1), seq) // MBLK
+    key_block = lax.broadcasted_iota(jnp.int32, (seq, pair * seq), 0) // MBLK
     mask_blocks = seq // MBLK
     all_blocks = 2 * half_blocks
     per = q_rows.shape[0]
@@ -217,7 +238,11 @@
         )
 
     def sample(m, carry):
-        rows = pl.ds(pl.multiple_of(m * seq, seq), seq)
+        rows = sample_rows(m)
+
+        @pl.when(pipe == 0)
+        def _():
+            got(u_buf.at[pl.ds((1 - t) * half_blocks, half_blocks), rows], tk_recv.at[m])
 
         @pl.when(pipe > 0)
         def _():
@@ -239,10 +264,10 @@
             values = u_buf[b, rows, :].astype(jnp.float32)
             normed[b] = (values * inv_rms * gain[:, b * BS : (b + 1) * BS]).astype(jnp.bfloat16)
 
-        allowed = jnp.zeros((seq, seq), jnp.int32)
+        allowed = jnp.zeros((seq, pair * seq), jnp.int32)
         for i in range(mask_blocks):
             for jj in range(mask_blocks):
-                here = (sublanes == i) & (lanes == jj)
+                here = (query_block == i) & (key_block == jj)
                 allowed = jnp.where(here, mask[m, i, jj], allowed)
 
         def project(mat, table, c):
@@ -256,24 +281,36 @@
             return acc.astype(jnp.bfloat16)
 
         def column(c, inner):
-            queries = project(0, q_rows, c)
-            keys = project(1, k_rows, c)
-            values = project(2, v_rows, c)
-            for head in range(BS // HD):
-                cut = slice(head * HD, (head + 1) * HD)
-                scores = lax.dot_general(
-                    queries[:, cut], keys[:, cut], nt, preferred_element_type=jnp.float32
-                ) * HD ** (-0.5)
-                scores = jnp.where(allowed == 1, scores, jnp.float32(-1e30))
-                top = jnp.max(scores, axis=-1, keepdims=True)
-                exps = jnp.exp(scores - top)
-                probs = (exps / jnp.sum(exps, axis=-1, keepdims=True)).astype(jnp.bfloat16)
-                att[c, :, cut] = jnp.dot(
-                    probs, values[:, cut], preferred_element_type=jnp.float32
-                ).astype(jnp.bfloat16)
+            for mat, table in enumerate((q_rows, k_rows, v_rows)):
+                heads[mat, c] = project(mat, table, c)
             return inner
 
-        lax.fori_loop(0, columns, column, 0, unroll=2)
+        lax.fori_loop(0, columns, column, 0, unroll=UNROLL_P)
+
+        def attend(c, inner):
+            queries, keys, values = heads[0, c], heads[1, c], heads[2, c]
+            empty = jnp.zeros((seq, HD), jnp.bfloat16)
+            spread = jnp.concatenate(
+                [
+                    jnp.concatenate([queries[:, :HD], empty], axis=1),
+                    jnp.concatenate([empty, queries[:, HD:]], axis=1),
+                ],
+                axis=0,
+            )
+            scores = lax.dot_general(
+                keys, spread, nt, preferred_element_type=jnp.float32
+            ) * HD ** (-0.5)
+            scores = jnp.where(allowed == 1, scores, jnp.float32(-1e30))
+            top = jnp.max(scores, axis=0, keepdims=True)
+            exps = jnp.exp(scores - top)
+            probs = (exps / jnp.sum(exps, axis=0, keepdims=True)).astype(jnp.bfloat16)
+            mixed = lax.dot_general(
+                probs, values, (((0,), (0,)), ((), ())), preferred_element_type=jnp.float32
+            ).astype(jnp.bfloat16)
+            att[c] = jnp.concatenate([mixed[:seq, :HD], mixed[seq:, HD:]], axis=1)
+            return inner
+
+        lax.fori_loop(0, columns, attend, 0, unroll=UNROLL_A)
 
         picks = o_rows.shape[0]
 
@@ -317,7 +354,12 @@
     lax.fori_loop(0, samples, sample, 0)
 
     def drain(m, carry):
-        rows = pl.ds(pl.multiple_of(m * seq, seq), seq)
+        rows = sample_rows(m)
+
+        @pl.when(pipe == 0)
+        def _():
+            got(u_buf.at[pl.ds(t * half_blocks, half_blocks), rows], tk_send.at[m])
+
         for j in range(chunks):
             rs_copy(m, j, rows).wait_send()
 
@@ -358,18 +400,21 @@
     ]
     blocks, depth, _ = shards[0].shape
     vmem = pl.BlockSpec(memory_space=pltpu.VMEM)
+    hbm = pl.BlockSpec(memory_space=pl.ANY)
     smem = pl.BlockSpec(memory_space=pltpu.SMEM)
     dma = pltpu.SemaphoreType.DMA
     result = pl.pallas_call(
         functools.partial(kernel, (nz, samples, seq)),
         out_shape=jax.ShapeDtypeStruct((half, row_count, BS), jnp.bfloat16),
-        in_specs=[vmem] * 6 + [smem] * 5,
+        in_specs=[hbm, vmem] + [hbm] * 4 + [smem] * 5,
         out_specs=vmem,
         scratch_shapes=[
             pltpu.VMEM((MATS, blocks, BS, BS), jnp.bfloat16),
             pltpu.VMEM((MATS, blocks // 2, depth, BS), jnp.bfloat16),
+            pltpu.VMEM((MATS, blocks // 2, depth, BS), jnp.bfloat16),
             pltpu.VMEM((2 * half, row_count, BS), jnp.bfloat16),
             pltpu.VMEM((2 * half, seq, BS), jnp.bfloat16),
+            pltpu.VMEM((3, half, seq, BS), jnp.bfloat16),
             pltpu.VMEM((half, seq, BS), jnp.bfloat16),
             pltpu.VMEM((half, seq, BS), jnp.float32),
             pltpu.VMEM((half, row_count, BS), jnp.bfloat16),
@@ -379,12 +424,14 @@
             dma((MATS,)),
             dma((MATS,)),
             dma((MATS,)),
+            dma((MATS,)),
             dma((MATS, nz)),
             dma((2, MATS)),
             dma((2, 2, MATS, nz // 2)),
             dma((MATS,)),
             dma((MATS,)),
-            dma((half,)),
+            dma((samples,)),
+            dma((samples,)),
             dma((half,)),
             dma((samples, 2)),
             dma((samples, 2)),

time: 225 us -> 184 us (0.82)
  Pallas kernels: 216 us -> 176 us
    pallas_call x1, Pallas kernels: 216 us -> 176 us  [body(): pl.pallas_call(functools.partial(kernel, (nz, samples, seq)), out_shape=j...]
where the time goes in v2:
time: 184 us
  Pallas kernels  176 us (96%)
  local copies, waits for them, and re-layouts  7.86 us (4%)
    pallas_call x1, Pallas kernels, body(): pl.pallas_call(functools.partial(kernel, (nz, samples, seq)), out_shape=j...  176 us
    unnamed x22, local copies, waits for them, and re-layouts  6.18 us

profile of v2, /device:TPU:24, one launch (start us, length us, event | category | flops | bytes accessed | tf_op | source)
XLA Modules:
  0.0 183.7 jit_solution(14332347418346561834)
XLA Ops:
  0.0 0.0 copy-start.6
  0.0 0.0 copy-start.8
  0.0 0.0 copy-start.7
  0.0 0.0 copy-start.10
  0.0 0.7 copy-done.9
  0.7 0.0 copy-done.6
  0.7 0.0 copy-done.8
  0.7 0.0 copy-done.7
  0.7 0.0 copy-done.10
  0.7 0.0 copy-start
  0.7 1.1 copy-done
  1.9 0.0 copy-start.1
  1.9 0.9 copy-done.1
  2.8 0.0 copy-start.2
  2.8 0.9 copy-done.2
  3.7 0.0 copy-start.3
  3.7 0.9 copy-done.3
  4.6 0.0 copy-start.4
  4.6 0.9 copy-done.4
  5.5 0.0 copy-start.5
  5.5 0.7 copy-done.5
  6.2 175.8 %shard_map.109 = bf16[8,192,256]{2,1,0:T(8,128)(2,1)S(1)} custom-call(bf16[192,2048]{1,0:T(8,128)(2,1)S(1)} %copy-done, f32[1,4096]{1,0:T(1,128)S(1)} %copy-done.5, bf16[32,8,256]{2,1,0:T(8,128)(2,1)S(1)} %bitcast.10, bf16[32,8,256]{2,1,0:T(8,128)(2,1)S(1)} %bitcast.11, bf16[32,8,256]{2,1,0:T(8,128)(2,1)S(1)} %bitcast.12, bf16[32,8,256]{2,1,0:T(8,128)(2,1)S(1)} %bitcast.13, ...), custom_call_target="tpu_custom_call" | custom-call | tf_op jit(solution)/shard_map/pallas_call | solution.py:406
  182.1 0.4 copy.12
  182.5 1.2 reshape.19
  (1 shorter events, 0.0 us)
Async XLA Ops:
  0.0 0.7 copy-start.9
  0.0 0.7 copy-start.6
  0.0 0.7 copy-start.8
  0.0 0.7 copy-start.7
  0.0 0.7 copy-start.10
  0.7 1.1 copy-start
  1.9 0.9 copy-start.1
  2.8 0.9 copy-start.2
  3.7 0.9 copy-start.3
  4.6 0.9 copy-start.4
  5.5 0.7 copy-start.5
